TPU v7x, 512 devices: a whole 4x8x8 slice. The times are simulated.
512 devices in a mesh: seq: 64 (over y, z), trk: 8 (over x, core).
Axes of the slice: x: 4, y: 8, z: 8, core: 2. Of those that a mesh axis runs over, the one named last changes fastest.
Arguments:
- embeddings: bfloat16 [4, 8192, 1920], P(None, 'seq', 'trk'), may hold values from -16 to 16
- head: bfloat16 [1920, 4096], P(None, 'trk'), may hold values from -0.125 to 0.125
- exon_starts: int32 [4, 128, 8], replicated, may hold values from 0 to 8184, as said below
- exon_lengths: int32 [4, 128, 8], replicated, may hold values from 1 to 8, as said below
- gene_owner: int32 [4, 128], replicated, may hold values from 0 to 63, as said below
- gene_targets: float32 [4, 256, 4096], P(None, 'seq', 'trk'), may hold values from 2 to 400, as said below
Outputs:
- gene_pred: float32 [4, 256, 4096], P(None, 'seq', 'trk')
- loss: float32 [4, 4096], P(None, 'trk')
- grad_head: float32 [1920, 4096], P('seq', 'trk')
Inputs may be any that keep to these rules, and one draw needn't show every extreme that they name: `exon_starts`: each gene has 8 exon blocks; blocks may intersect. Some block of each window starts at 0 and some at 8184. `exon_lengths`: some block of each window has length 8. `gene_owner`: in each window no owner holds more than 4 genes, and some owner holds exactly 4. `gene_targets`: entries of empty slots are read by nothing.
All inputs are finite; a program needn't handle non-finite values.
Results may differ from a plain program's by a relative error of at most 0.0041.
Values may be sent and summed in bfloat16 or wider, within the bound.
No kernel may reach another device: no remote copies, remote signals or barrier semaphores. Data moves between devices by JAX's collectives and lax.ppermute only.
A program may use at most 64 MiB of HBM per device.

v0:
```python
import jax
import jax.numpy as jnp
from jax import lax
from jax.sharding import PartitionSpec as P


def slot_table(gene_owner, capacity):
    genes = gene_owner.shape[1]
    same = gene_owner[:, :, None] == gene_owner[:, None, :]
    earlier = jnp.arange(genes)[None, :] < jnp.arange(genes)[:, None]
    ahead = jnp.sum((same & earlier[None]).astype(jnp.int32), axis=2)
    return gene_owner * capacity + ahead


def coverage(starts, lengths, positions):
    where_bin = positions[None, None, None, :]
    inside = (where_bin >= starts[..., None]) & (where_bin < (starts + lengths)[..., None])
    return jnp.sum(inside.astype(jnp.float32), axis=2)


def fold_sources(received):
    return jnp.sum(received, axis=1)


def per_device(embeddings, head, exon_starts, exon_lengths, gene_owner, gene_targets):
    seq_devices = lax.axis_size("seq")
    seq_place = lax.axis_index("seq")
    windows, bin_dev, _ = embeddings.shape
    genes = gene_owner.shape[1]
    capacity = gene_targets.shape[1]
    slot_total = seq_devices * capacity
    whole = lax.all_gather(embeddings, "trk", axis=2, tiled=True)
    logits = jnp.einsum("wbd,dt->wbt", whole, head, preferred_element_type=jnp.float32)
    pred = jax.nn.softplus(logits).astype(jnp.bfloat16)
    positions = seq_place * bin_dev + jnp.arange(bin_dev, dtype=jnp.int32)
    cover = coverage(exon_starts, exon_lengths, positions)
    slot_of = slot_table(gene_owner, capacity)
    onehot = (slot_of[..., None] == jnp.arange(slot_total, dtype=jnp.int32)).astype(jnp.float32)
    member = jnp.einsum("wgs,wgb->wsb", onehot, cover, precision=lax.Precision.HIGHEST).astype(
        jnp.bfloat16
    )
    valid = jnp.sum(onehot, axis=1)
    valid_here = lax.dynamic_slice_in_dim(valid, seq_place * capacity, capacity, 1)
    targets_here = gene_targets * valid_here[..., None]
    target_part = jnp.sum(targets_here, axis=1)
    partial_value = jnp.einsum("wsb,wbt->wst", member, pred, preferred_element_type=jnp.float32)
    blocks = partial_value.reshape(windows, seq_devices, capacity, partial_value.shape[2])
    gene_here = fold_sources(lax.all_to_all(blocks, "seq", split_axis=1, concat_axis=1, tiled=True))
    safe = jnp.where(valid_here[..., None] > 0, gene_here, 1.0)
    fit_part = jnp.sum(targets_here * jnp.log(safe), axis=1)
    total, target_sum, fit = lax.psum((jnp.sum(gene_here, axis=1), target_part, fit_part), "seq")
    scale_rows = (genes / target_sum)[:, None, :]
    gene_grad = (
        scale_rows
        * (
            valid_here[..., None] * (0.2 + 0.8 * target_sum / total)[:, None, :]
            - targets_here / safe
        )
    ).astype(jnp.bfloat16)
    bin_grad = jnp.einsum(
        "wsb,wst->wbt",
        member,
        lax.all_gather(gene_grad, "seq", axis=1, tiled=True),
        preferred_element_type=jnp.float32,
    )
    logit_grad = (bin_grad * jax.nn.sigmoid(logits)).astype(jnp.bfloat16)
    grad_head = lax.psum_scatter(
        jnp.einsum("wbd,wbt->dt", whole, logit_grad, preferred_element_type=jnp.float32),
        "seq",
        scatter_dimension=0,
        tiled=True,
    )
    log_total = jnp.log(total)
    loss = (-fit + target_sum * log_total + 0.2 * (total - target_sum * log_total)) / target_sum
    return (gene_here, loss, grad_head)


def solution(mesh):
    return jax.shard_map(
        per_device,
        mesh=mesh,
        in_specs=(P(None, "seq", "trk"), P(None, "trk"), P(), P(), P(), P(None, "seq", "trk")),
        out_specs=(P(None, "seq", "trk"), P(None, "trk"), P("seq", "trk")),
        check_vma=False,
    )
```

profile of v0, /device:TPU:2, one launch (start us, length us, event | category | flops | bytes accessed | tf_op | source)
XLA Modules:
  0.0 664.6 jit_solution(17121487797619391338)
XLA Ops:
  7.2 0.0 all-gather.3.cloned.1.call-start
  7.2 0.7 all-gather.3.cloned.1.call-update
  7.9 0.8 copy.28
  8.8 0.7 add.46
  9.5 0.1 copy.29
  9.7 1.0 convert_reduce_fusion.2
  10.7 0.7 multiply_add_fusion
  11.4 1.4 convert_reduce_fusion
  12.8 0.4 convolution_convert_fusion
  13.2 30.7 %all-gather.3.cloned.1.call-done = bf16[4,128,1920]{1,2,0:T(8,128)(2,1)} async-done(((bf16[4,128,240]{1,2,0:T(8,128)(2,1)}), bf16[4,128,1920]{1,2,0:T(8,128)(2,1)}) %all-gather.3.cloned.1.call-update) | async-done | bytes 1966096 | tf_op jit(solution)/shard_map/all_gather | solution.py:32
  43.9 2.8 fusion.13
  46.8 2.2 fusion.9
  48.9 2.9 reshape.35
  51.8 3.5 copy.30
  55.4 13.6 %all-to-all-start = ((f32[4,64,4,512]{3,2,0,1:T(4,128)}), f32[4,64,4,512]{3,2,0,1:T(4,128)}, u32[]{:S(2)}, u32[]{:S(2)}) async-start(f32[4,64,4,512]{3,2,0,1:T(4,128)} %copy.30), calls=%async_computation | async-start | bytes 4194304 | tf_op jit(solution)/shard_map/all_to_all | solution.py:48
  68.9 0.0 all-gather.5.cloned.1.call-start
  69.0 0.1 convert_reduce_fusion.1
  69.1 0.1 broadcast_compare_fusion
  69.2 51.5 %all-to-all-done = f32[4,64,4,512]{3,2,0,1:T(4,128)} async-done(((f32[4,64,4,512]{3,2,0,1:T(4,128)}), f32[4,64,4,512]{3,2,0,1:T(4,128)}, u32[]{:S(2)}, u32[]{:S(2)}) %all-to-all-start) | async-done | bytes 2097184 | tf_op jit(solution)/shard_map/all_to_all | solution.py:48
  120.7 2.1 fusion.20
  122.8 0.1 multiply_reduce_fusion
  122.9 282.3 %all-reduce.1 = (f32[4,512]{1,0:T(4,128)S(1)}, f32[4,512]{1,0:T(4,128)S(1)}, f32[4,512]{1,0:T(4,128)S(1)}) all-reduce(f32[4,512]{1,0:T(4,128)S(1)} %get-tuple-element.18, f32[4,512]{1,0:T(4,128)S(1)} %get-tuple-element.15, f32[4,512]{1,0:T(4,128)S(1)} %get-tuple-element.17), channel_id=1, replica_groups=mesh['seq'=64,'trk'=8] {'seq'}, use_global_device_ids=true, to_apply=%region_7.8 | all-reduce | flops 6144 | bytes 49152 | tf_op jit(solution)/shard_map/psum | solution.py:51
  405.2 0.6 fusion.16
  405.8 0.1 multiply_convert_fusion
  405.9 0.6 copy.31
  406.5 0.0 all-reduce.4.cloned.1.call-start
  406.6 76.9 %all-gather.5.cloned.1.call-done = bf16[4,256,512]{2,0,1:T(4,128)(2,1)} async-done(((bf16[4,4,512]{2,0,1:T(4,128)(2,1)}), bf16[4,256,512]{2,0,1:T(4,128)(2,1)}) %all-gather.5.cloned.1.call-update) | async-done | bytes 1048592 | tf_op jit(solution)/shard_map/all_gather | solution.py:63
  483.5 5.5 convolution_bitcast_fusion
  489.0 1.3 dynamic-slice
  490.9 165.2 %all-reduce.4.cloned.1.call-done = f32[1920,512]{0,1:T(8,128)} async-done(((f32[1920,512]{0,1:T(8,128)}), f32[1920,512]{0,1:T(8,128)}) %all-reduce.4.cloned.1.call-update) | async-done | bytes 3932176
  656.1 1.2 constant_dynamic-slice_fusion
  657.3 0.8 copy.35
  (10 shorter events, 0.1 us)
Async XLA Ops:
  7.2 36.7 %copy-start = (bf16[1920,512]{1,0:T(8,128)(2,1)S(1)}, bf16[1920,512]{1,0:T(8,128)(2,1)}, u32[]{:S(2)}) copy-start(bf16[1920,512]{1,0:T(8,128)(2,1)} %param.7) | copy-start | bytes 5898244
  7.2 36.7 %all-gather.3.cloned.1.call-start = ((), (), s32[]{:S(2)}) async-start(), calls=%async_computation.1 | async-start | bytes 2211840 | tf_op jit(solution)/shard_map/all_gather | solution.py:32
  55.4 65.3 %all-to-all-start = ((f32[4,64,4,512]{3,2,0,1:T(4,128)}), f32[4,64,4,512]{3,2,0,1:T(4,128)}, u32[]{:S(2)}, u32[]{:S(2)}) async-start(f32[4,64,4,512]{3,2,0,1:T(4,128)} %copy.30), calls=%async_computation | async-start | bytes 4194304 | tf_op jit(solution)/shard_map/all_to_all | solution.py:48
  68.9 53.8 %copy-start.2 = (f32[4,4,512]{2,1,0:T(4,128)S(1)}, f32[4,4,512]{2,1,0:T(4,128)}, u32[]{:S(2)}) copy-start(f32[4,4,512]{2,1,0:T(4,128)} %param.11) | copy-start | bytes 98308
  68.9 414.6 %all-gather.5.cloned.1.call-start = ((), (), s32[]{:S(2)}) async-start(), calls=%async_computation.2 | async-start | bytes 1064960 | tf_op jit(solution)/shard_map/all_gather | solution.py:63
  122.7 366.2 %copy-start.1 = (f32[4,4,512]{2,1,0:T(4,128)}, f32[4,4,512]{2,1,0:T(4,128)S(1)}, u32[]{:S(2)}) copy-start(f32[4,4,512]{2,1,0:T(4,128)S(1)} %get-tuple-element.16) | copy-start | bytes 98308
  406.5 249.6 %all-reduce.4.cloned.1.call-start = ((), (), s32[]{:S(2)}) async-start(), calls=%async_computation.3 | async-start | bytes 7864320
Sparse Core Ops, SparseCore 0:
  10.1 33.7 all-gather.2
  406.7 76.7 all-gather.4
  489.1 166.9 all-reduce.3
where the time goes:
time: 665 us
  waiting for transfers between devices  325 us (49%)
  blocking collectives  282 us (42%)
  between operations  14.5 us (2%)
  starting transfers between devices  13.7 us (2%)
  local copies, waits for them, and re-layouts  11.2 us (2%)
  matrix products  10.9 us (2%)
  other arithmetic  7 us (1%)
    psum x1, blocking collectives, per_device(): lax.psum((jnp.sum(gene_here, axis=1), target_part, fit_part), 'seq')  282 us
    unnamed x4, waiting for transfers between devices  166 us
    all_gather x1, waiting for transfers between devices, per_device(): lax.all_gather(gene_grad, 'seq', axis=1, tiled=True)  76.9 us
    all_to_all x1, waiting for transfers between devices, per_device(): lax.all_to_all(blocks, 'seq', split_axis=1, concat_axis=1, tiled=True)  51.5 us
    all_gather x1, waiting for transfers between devices, per_device(): whole = lax.all_gather(embeddings, 'trk', axis=2, tiled=True)  30.7 us
    all_to_all x1, starting transfers between devices, per_device(): lax.all_to_all(blocks, 'seq', split_axis=1, concat_axis=1, tiled=True)  13.6 us
  transfers between devices with their start and end apart: 4, of which 4 were waited for; matrix products, arithmetic and copies ran while one was open for 1% of the time, Pallas kernels for 0%

commit v1 on v0

--- a/solution.py
+++ b/solution.py
@@ -2,6 +2,12 @@
 import jax.numpy as jnp
 from jax import lax
 from jax.sharding import PartitionSpec as P
+
+
+def gather_from_all(x, axis, dim):
+    size = lax.axis_size(axis)
+    repeats = [size if d == dim else 1 for d in range(x.ndim)]
+    return lax.all_to_all(jnp.tile(x, repeats), axis, split_axis=dim, concat_axis=dim, tiled=True)
 
 
 def slot_table(gene_owner, capacity):
@@ -60,7 +66,7 @@
     bin_grad = jnp.einsum(
         "wsb,wst->wbt",
         member,
-        lax.all_gather(gene_grad, "seq", axis=1, tiled=True),
+        gather_from_all(gene_grad, "seq", 1),
         preferred_element_type=jnp.float32,
     )
     logit_grad = (bin_grad * jax.nn.sigmoid(logits)).astype(jnp.bfloat16)

time: 665 us -> 615 us (0.925)
  waiting for transfers between devices: 325 us -> 246 us
  blocking collectives: 282 us -> 311 us
    all_gather x1 -> x0, waiting for transfers between devices: 76.9 us -> none  [per_device(): lax.all_gather(gene_grad, 'seq', axis=1, tiled=True)]
    all_to_all x0 -> x1, blocking collectives: none -> 26.6 us  [gather_from_all(): lax.all_to_all(jnp.tile(x, repeats), axis, split_axis=dim, concat_axis=di...]
    unnamed x4 -> x3, waiting for transfers between devices: 166 us -> 164 us
  transfers between devices with their start and end apart: 4 -> 3, of which waited for: 4 -> 3; matrix products, arithmetic and copies ran while one was open for 1% -> 1% of each run, Pallas kernels for 0% -> 0%
where the time goes in v1:
time: 615 us
  blocking collectives  311 us (51%)
  waiting for transfers between devices  246 us (40%)
  between operations  14.8 us (2%)
  starting transfers between devices  13.6 us (2%)
  local copies, waits for them, and re-layouts  11.1 us (2%)
  matrix products  10.9 us (2%)
  other arithmetic  7 us (1%)
    psum x1, blocking collectives, per_device(): lax.psum((jnp.sum(gene_here, axis=1), target_part, fit_part), 'seq')  285 us
    unnamed x3, waiting for transfers between devices  164 us
    all_to_all x1, waiting for transfers between devices, per_device(): lax.all_to_all(blocks, 'seq', split_axis=1, concat_axis=1, tiled=True)  51.5 us
    all_gather x1, waiting for transfers between devices, per_device(): whole = lax.all_gather(embeddings, 'trk', axis=2, tiled=True)  30.7 us
    all_to_all x1, blocking collectives, gather_from_all(): lax.all_to_all(jnp.tile(x, repeats), axis, split_axis=dim, concat_axis=di...  26.6 us
    all_to_all x1, starting transfers between devices, per_device(): lax.all_to_all(blocks, 'seq', split_axis=1, concat_axis=1, tiled=True)  13.6 us
  transfers between devices with their start and end apart: 3, of which 3 were waited for; matrix products, arithmetic and copies ran while one was open for 1% of the time, Pallas kernels for 0%

profile of v1, /device:TPU:2, one launch (start us, length us, event | category | flops | bytes accessed | tf_op | source)
XLA Modules:
  0.0 614.8 jit_solution(17201438990222543362)
XLA Ops:
  7.2 0.0 all-gather.2.cloned.1.call-start
  7.2 0.7 all-gather.2.cloned.1.call-update
  7.9 0.8 copy.19
  8.8 0.7 add.46
  9.5 0.1 copy.20
  9.7 1.0 convert_reduce_fusion.2
  10.7 0.7 multiply_add_fusion
  11.4 1.4 convert_reduce_fusion
  12.8 0.4 convolution_convert_fusion
  13.2 30.7 %all-gather.2.cloned.1.call-done = bf16[4,128,1920]{1,2,0:T(8,128)(2,1)} async-done(((bf16[4,128,240]{1,2,0:T(8,128)(2,1)}), bf16[4,128,1920]{1,2,0:T(8,128)(2,1)}) %all-gather.2.cloned.1.call-update) | async-done | bytes 1966096 | tf_op jit(solution)/shard_map/all_gather | solution.py:38
  43.9 2.8 fusion.13
  46.8 2.2 fusion.9
  48.9 2.9 reshape.39
  51.8 3.5 copy.21
  55.4 13.6 %all-to-all-start = ((f32[4,64,4,512]{3,2,0,1:T(4,128)}), f32[4,64,4,512]{3,2,0,1:T(4,128)}, u32[]{:S(2)}, u32[]{:S(2)}) async-start(f32[4,64,4,512]{3,2,0,1:T(4,128)} %copy.21), calls=%async_computation | async-start | bytes 4194304 | tf_op jit(solution)/shard_map/all_to_all | solution.py:54
  68.9 0.0 all-reduce.4.cloned.1.call-start
  69.0 0.1 convert_reduce_fusion.1
  69.1 0.1 broadcast_compare_fusion
  69.2 51.5 %all-to-all-done = f32[4,64,4,512]{3,2,0,1:T(4,128)} async-done(((f32[4,64,4,512]{3,2,0,1:T(4,128)}), f32[4,64,4,512]{3,2,0,1:T(4,128)}, u32[]{:S(2)}, u32[]{:S(2)}) %all-to-all-start) | async-done | bytes 2097184 | tf_op jit(solution)/shard_map/all_to_all | solution.py:54
  120.7 2.1 fusion.20
  122.8 0.1 multiply_reduce_fusion
  122.9 284.7 %all-reduce.1 = (f32[4,512]{1,0:T(4,128)S(1)}, f32[4,512]{1,0:T(4,128)S(1)}, f32[4,512]{1,0:T(4,128)S(1)}) all-reduce(f32[4,512]{1,0:T(4,128)S(1)} %get-tuple-element.15, f32[4,512]{1,0:T(4,128)S(1)} %get-tuple-element.12, f32[4,512]{1,0:T(4,128)S(1)} %get-tuple-element.14), channel_id=1, replica_groups=mesh['seq'=64,'trk'=8] {'seq'}, use_global_device_ids=true, to_apply=%region_7.8 | all-reduce | flops 6144 | bytes 49152 | tf_op jit(solution)/shard_map/psum | solution.py:57
  407.6 0.6 fusion.16
  408.2 0.1 multiply_convert_fusion
  408.3 0.5 tile.4
  408.8 26.6 %all_to_all.10 = bf16[4,256,512]{2,0,1:T(4,128)(2,1)} all-to-all(bf16[4,256,512]{2,0,1:T(4,128)(2,1)S(1)} %bitcast.18), channel_id=1, replica_groups=mesh['seq'=64,'trk'=8] {'seq'}, dimensions={1} | all-to-all | bytes 2097152 | tf_op jit(solution)/shard_map/all_to_all | solution.py:10
  435.5 5.5 convolution_bitcast_fusion
  441.0 0.0 all-reduce.4.cloned.1.call-update
  441.0 1.3 dynamic-slice
  442.9 163.1 %all-reduce.4.cloned.1.call-done = f32[1920,512]{0,1:T(8,128)} async-done(((f32[1920,512]{0,1:T(8,128)}), f32[1920,512]{0,1:T(8,128)}) %all-reduce.4.cloned.1.call-update) | async-done | bytes 3932176
  606.0 1.2 constant_dynamic-slice_fusion
  607.2 0.8 copy.26
  (9 shorter events, 0.1 us)
Async XLA Ops:
  7.2 36.7 %copy-start = (bf16[1920,512]{1,0:T(8,128)(2,1)S(1)}, bf16[1920,512]{1,0:T(8,128)(2,1)}, u32[]{:S(2)}) copy-start(bf16[1920,512]{1,0:T(8,128)(2,1)} %param.7) | copy-start | bytes 5898244
  7.2 36.7 %all-gather.2.cloned.1.call-start = ((), (), s32[]{:S(2)}) async-start(), calls=%async_computation.2 | async-start | bytes 2211840 | tf_op jit(solution)/shard_map/all_gather | solution.py:38
  55.4 65.3 %all-to-all-start = ((f32[4,64,4,512]{3,2,0,1:T(4,128)}), f32[4,64,4,512]{3,2,0,1:T(4,128)}, u32[]{:S(2)}, u32[]{:S(2)}) async-start(f32[4,64,4,512]{3,2,0,1:T(4,128)} %copy.21), calls=%async_computation | async-start | bytes 4194304 | tf_op jit(solution)/shard_map/all_to_all | solution.py:54
  68.9 53.8 %copy-start.2 = (f32[4,4,512]{2,1,0:T(4,128)S(1)}, f32[4,4,512]{2,1,0:T(4,128)}, u32[]{:S(2)}) copy-start(f32[4,4,512]{2,1,0:T(4,128)} %param.11) | copy-start | bytes 98308
  68.9 537.1 %all-reduce.4.cloned.1.call-start = ((), (), s32[]{:S(2)}) async-start(), calls=%async_computation.3 | async-start | bytes 7864320
  122.7 318.2 %copy-start.1 = (f32[4,4,512]{2,1,0:T(4,128)}, f32[4,4,512]{2,1,0:T(4,128)S(1)}, u32[]{:S(2)}) copy-start(f32[4,4,512]{2,1,0:T(4,128)S(1)} %get-tuple-element.13) | copy-start | bytes 98308
Sparse Core Ops, SparseCore 0:
  10.1 33.7 all-gather.1
  441.1 164.8 all-reduce.3
